TPU v7x, 256 devices: a whole 4x4x8 slice. The times are simulated.
256 devices in a mesh: kv: 8 (over x, core), seq: 8 (over z), vocab: 4 (over y).
Axes of the slice: x: 4, y: 4, z: 8, core: 2. Of those that a mesh axis runs over, the one named last changes fastest.
Arguments:
- hidden_state: bfloat16 [48, 4, 3584], P('kv', 'vocab', 'seq'), may hold values from -6 to 6
- input_projection: bfloat16 [3584, 8, 1024], P('seq', 'kv'), may hold values from -0.09375 to 0.09375
- output_projection: bfloat16 [8, 512, 3584], P('kv', None, 'seq'), may hold values from -0.09375 to 0.09375
- norm_pre_attention: float32 [3584], P('seq'), may hold values from 0.1 to 1.9
- norm_post_attention: float32 [3584], P('seq'), may hold values from 0.1 to 1.9
- norm_pre_feedforward: float32 [3584], P('seq'), may hold values from 0.1 to 1.9
- norm_post_feedforward: float32 [3584], P('seq'), may hold values from 0.1 to 1.9
- norm_final: float32 [3584], P('seq'), may hold values from 0.1 to 1.9
- cache_keys: bfloat16 [4, 16384, 8, 256], P('vocab', 'seq', 'kv')
- cache_values: bfloat16 [4, 16384, 8, 256], P('vocab', 'seq', 'kv')
- cache_length: int32 [4], P('vocab'), may hold values from 1 to 16379, as said below
- ancestors: int32 [4, 48, 48], P('vocab'), may hold values from 0 to 1, as said below
- accepted_path: int32 [4, 5], P('vocab'), may hold values from 0 to 47, as said below
- gate_up_weight: bfloat16 [3584, 2, 14336], P('seq', None, ('kv', 'vocab')), may hold values from -0.09375 to 0.09375
- down_weight: bfloat16 [14336, 3584], P(('kv', 'vocab'), 'seq'), may hold values from -0.046875 to 0.046875
- draft_weight: bfloat16 [4, 3584, 3584], P(None, 'seq', ('kv', 'vocab')), may hold values from -0.09375 to 0.09375
- draft_bias: float32 [4, 3584], P(None, ('kv', 'vocab')), may hold values from -3 to 3
- vocab_weight: bfloat16 [131072, 3584], P(('kv', 'seq', 'vocab'))
- candidate_tokens: int32 [5, 48, 4, 8], replicated, may hold values from 0 to 131071
Outputs:
- keys_updated: bfloat16 [4, 16384, 8, 256], P('vocab', 'seq', 'kv')
- values_updated: bfloat16 [4, 16384, 8, 256], P('vocab', 'seq', 'kv')
- log_normalizer: float32 [5, 48, 4], replicated
- candidate_logits: float32 [5, 48, 4, 8], replicated
Inputs may be any that keep to these rules, and one draw needn't show every extreme that they name: The first cache_length[k] slots of tenant k's cache are filled; in every draw some tenant holds exactly 16379. ancestors[k, t, u] is 1 exactly when u is t or an ancestor of t in tenant k's tree; node 0 is the root and every parent has a lower index than its child. accepted_path[k] lists 5 nodes of tenant k's tree from the root down, each the parent of the next; the last of them is node 47.
All inputs are finite; a program needn't handle non-finite values.
Results may differ from a plain program's by a relative error of at most 0.02.
Values may be sent and summed in bfloat16 or wider, within the bound.
A program may use at most 64 MiB of HBM per device.

v0:
```python
import jax
import jax.numpy as jnp
from jax import lax
from jax.sharding import PartitionSpec as P

MODEL_WIDTH = 3584
HEAD_SIZE = 256
CAND = 8
EPSILON = 1e-06
SCORE_CAP = 50.0
LOGIT_CAP = 30.0


def apply_rotary(vectors, token_positions):
    half_dim = vectors.shape[-1] // 2
    frequency = 10000.0 ** (-2.0 * jnp.arange(half_dim, dtype=jnp.float32) / vectors.shape[-1])
    angles = token_positions.astype(jnp.float32)[..., None] * frequency
    cosine = jnp.cos(angles)
    sine_part = jnp.sin(angles)
    first_half = vectors[..., :half_dim]
    second_half = vectors[..., half_dim:]
    return jnp.concatenate(
        [
            first_half * cosine - second_half * sine_part,
            second_half * cosine + first_half * sine_part,
        ],
        axis=-1,
    )


def capped_weight(scores):
    return jnp.exp(SCORE_CAP * jnp.tanh(scores * 0.0625 / SCORE_CAP))


def row_inverse(values):
    totals = lax.psum(jnp.sum(values * values, axis=-1), "seq")
    return lax.rsqrt(totals / MODEL_WIDTH + EPSILON)[:, None]


def gated_units(gate_up, squares):
    inverse = lax.rsqrt(squares / MODEL_WIDTH + EPSILON)[:, None]
    return (
        jax.nn.gelu(gate_up[:, 0] * inverse, approximate=True) * (gate_up[:, 1] * inverse)
    ).astype(jnp.bfloat16)


def local(
    hidden_state,
    input_projection,
    output_projection,
    norm_pre_attention,
    norm_post_attention,
    norm_pre_feedforward,
    norm_post_feedforward,
    norm_final,
    cache_keys,
    cache_values,
    cache_length,
    ancestors,
    accepted_path,
    gate_up_weight,
    down_weight,
    draft_weight,
    draft_bias,
    vocab_weight,
    candidate_tokens,
):
    tok_block = hidden_state.shape[0]
    kv_count = lax.axis_size("kv")
    tenants = lax.axis_size("vocab")
    tree_size = tok_block * kv_count
    own_state = hidden_state[:, 0, :]
    tenant_state = lax.all_gather(own_state, "kv", axis=0, tiled=True)
    tenant_float = tenant_state.astype(jnp.float32)
    scaled_input = (tenant_float * norm_pre_attention).astype(jnp.bfloat16)
    projected_rows = jnp.einsum(
        "td,dhc->thc", scaled_input, input_projection, preferred_element_type=jnp.float32
    )
    projected_rows, squares = lax.psum(
        (projected_rows, jnp.sum(tenant_float * tenant_float, axis=-1)), "seq"
    )
    projected_rows = projected_rows * lax.rsqrt(squares / MODEL_WIDTH + EPSILON)[:, None, None]
    head_count = projected_rows.shape[1]
    depths = jnp.sum(ancestors[0], axis=-1) - 1
    length = cache_length[0]
    token_positions = length + depths
    query_rows = apply_rotary(
        projected_rows[:, :, : 2 * HEAD_SIZE].reshape(tree_size, head_count, 2, HEAD_SIZE),
        token_positions[:, None, None],
    ).astype(jnp.bfloat16)
    new_keys = apply_rotary(
        projected_rows[:, :, 2 * HEAD_SIZE : 3 * HEAD_SIZE], token_positions[:, None]
    ).astype(jnp.bfloat16)
    new_values = projected_rows[:, :, 3 * HEAD_SIZE :].astype(jnp.bfloat16)
    block_size = cache_keys.shape[1]
    block_start = lax.axis_index("seq") * block_size
    cache_cells = block_start + jnp.arange(block_size, dtype=jnp.int32)
    scores = jnp.einsum(
        "thgc,shc->thgs", query_rows, cache_keys[0], preferred_element_type=jnp.float32
    )
    weights = jnp.where((cache_cells < length)[None, None, None, :], capped_weight(scores), 0.0)
    numerator = jnp.einsum(
        "thgs,shc->thgc",
        weights.astype(jnp.bfloat16),
        cache_values[0],
        preferred_element_type=jnp.float32,
    )
    numerator, denominator = lax.psum((numerator, jnp.sum(weights, axis=-1)), "seq")
    tree_scores = jnp.einsum(
        "thgc,uhc->thgu", query_rows, new_keys, preferred_element_type=jnp.float32
    )
    tree_weights = jnp.where(ancestors[0][:, None, None, :] > 0, capped_weight(tree_scores), 0.0)
    numerator = numerator + jnp.einsum(
        "thgu,uhc->thgc",
        tree_weights.astype(jnp.bfloat16),
        new_values,
        preferred_element_type=jnp.float32,
    )
    denominator = denominator + jnp.sum(tree_weights, axis=-1)
    attended = (
        (numerator / denominator[..., None])
        .astype(jnp.bfloat16)
        .reshape(tree_size, head_count * 2 * HEAD_SIZE)
    )
    out_matrix = output_projection.reshape(head_count * 2 * HEAD_SIZE, output_projection.shape[2])
    attention_out = lax.psum_scatter(
        jnp.dot(attended, out_matrix, preferred_element_type=jnp.float32),
        "kv",
        scatter_dimension=0,
        tiled=True,
    )
    first_sum = (
        own_state.astype(jnp.float32)
        + attention_out * row_inverse(attention_out) * norm_post_attention
    ).astype(jnp.bfloat16)
    all_state = lax.all_gather(first_sum, ("kv", "vocab"), axis=0, tiled=True)
    all_float = all_state.astype(jnp.float32)
    scaled_ffn = (all_float * norm_pre_feedforward).astype(jnp.bfloat16)
    gate_up = jnp.einsum(
        "td,dcf->tcf", scaled_ffn, gate_up_weight, preferred_element_type=jnp.float32
    )
    ffn_squares = jnp.sum(all_float * all_float, axis=-1)
    gate_up, ffn_squares = lax.psum((gate_up, ffn_squares), "seq")
    activated = gated_units(gate_up, ffn_squares)
    ffn_out = lax.psum_scatter(
        jnp.dot(activated, down_weight, preferred_element_type=jnp.float32),
        ("kv", "vocab"),
        scatter_dimension=0,
        tiled=True,
    )
    first_float = first_sum.astype(jnp.float32)
    second_sum = (first_float + ffn_out * row_inverse(ffn_out) * norm_post_feedforward).astype(
        jnp.bfloat16
    )
    second_float = second_sum.astype(jnp.float32)
    normed = (second_float * row_inverse(second_float) * norm_final).astype(jnp.bfloat16)
    gathered = lax.all_gather(normed, ("kv", "vocab"), axis=0, tiled=True)
    lifted = jnp.einsum("td,ndc->tnc", gathered, draft_weight, preferred_element_type=jnp.float32)
    lifted = lax.psum(lifted.astype(jnp.bfloat16), "seq").astype(jnp.float32)
    branch = jax.nn.silu(lifted + draft_bias).astype(jnp.bfloat16)
    row_count = gathered.shape[0]
    vocab_rows = vocab_weight.shape[0]
    draft_count = branch.shape[1]
    columns = vocab_weight
    base_logits = lax.dot_general(
        lax.all_gather(gathered, "seq", axis=1, tiled=True),
        columns,
        (((1,), (1,)), ((), ())),
        preferred_element_type=jnp.float32,
    )
    columns = vocab_weight
    draft_extra = jnp.einsum(
        "tnc,vc->tnv",
        lax.all_gather(branch, ("kv", "vocab"), axis=2, tiled=True),
        columns,
        preferred_element_type=jnp.float32,
    )
    raw_logits = jnp.concatenate(
        [base_logits[:, None, :], base_logits[:, None, :] + draft_extra], axis=1
    )
    logits = LOGIT_CAP * jnp.tanh(raw_logits / LOGIT_CAP)
    totals = jnp.sum(jnp.exp(logits), axis=-1)
    head_total = draft_count + 1
    candidates = candidate_tokens.reshape(head_total, kv_count, tok_block, tenants, CAND)
    candidates = jnp.transpose(candidates, (0, 1, 3, 2, 4)).reshape(head_total, row_count, CAND)
    candidates = jnp.transpose(candidates, (1, 0, 2))
    vocab_start = lax.axis_index(("kv", "seq", "vocab")) * vocab_rows
    local_tokens = candidates - vocab_start
    entry_index = jnp.arange(vocab_rows, dtype=jnp.int32)
    picked = jnp.stack(
        [
            jnp.sum(
                jnp.where(entry_index == local_tokens[:, :, column : column + 1], logits, 0.0),
                axis=-1,
            )
            for column in range(CAND)
        ],
        axis=-1,
    )
    totals, picked = lax.psum((totals, picked), ("kv", "seq", "vocab"))
    log_totals = jnp.transpose(jnp.log(totals)).reshape(head_total, kv_count, tenants, tok_block)
    log_normalizer = jnp.transpose(log_totals, (0, 1, 3, 2)).reshape(head_total, tree_size, tenants)
    picked = jnp.transpose(picked, (1, 0, 2)).reshape(
        head_total, kv_count, tenants, tok_block, CAND
    )
    candidate_logits = jnp.transpose(picked, (0, 1, 3, 2, 4)).reshape(
        head_total, tree_size, tenants, CAND
    )
    accept_count = accepted_path.shape[1]
    slot_rows = length + jnp.arange(accept_count, dtype=jnp.int32)
    tree_nodes = jnp.arange(tree_size, dtype=jnp.int32)
    matches = (cache_cells[:, None, None] == slot_rows[None, :, None]) & (
        accepted_path[0][None, :, None] == tree_nodes[None, None, :]
    )
    selector = jnp.sum(matches.astype(jnp.float32), axis=1)
    written = jnp.sum(selector, axis=-1) > 0.0
    selector = selector.astype(jnp.bfloat16)

    def write_path(old_block, fresh_rows):
        moved_rows = jnp.dot(
            selector, fresh_rows.reshape(tree_size, -1), preferred_element_type=jnp.float32
        ).astype(jnp.bfloat16)
        return jnp.where(
            written[:, None], moved_rows, old_block[0].reshape(block_size, -1)
        ).reshape(old_block.shape)

    keys_updated = write_path(cache_keys, new_keys)
    values_updated = write_path(cache_values, new_values)
    return (keys_updated, values_updated, log_normalizer, candidate_logits)


def solution(mesh):
    placed = (
        P("kv", "vocab", "seq"),
        P("seq", "kv", None),
        P("kv", None, "seq"),
        P("seq"),
        P("seq"),
        P("seq"),
        P("seq"),
        P("seq"),
        P("vocab", "seq", "kv", None),
        P("vocab", "seq", "kv", None),
        P("vocab"),
        P("vocab", None, None),
        P("vocab", None),
        P("seq", None, ("kv", "vocab")),
        P(("kv", "vocab"), "seq"),
        P(None, "seq", ("kv", "vocab")),
        P(None, ("kv", "vocab")),
        P(("kv", "seq", "vocab"), None),
        P(),
    )
    return jax.shard_map(
        local,
        mesh=mesh,
        in_specs=placed,
        out_specs=(P("vocab", "seq", "kv", None), P("vocab", "seq", "kv", None), P(), P()),
        check_vma=False,
    )
```

profile of v0, /device:TPU:1, one launch (start us, length us, event | category | flops | bytes accessed | tf_op | source)
XLA Modules:
  0.0 775.7 jit_solution(17245792410160348582)
XLA Ops:
  8.1 15.8 %all-gather = bf16[48,1,448]{2,1,0:T(2,128)(2,1)S(1)} all-gather(bf16[6,1,448]{2,1,0:T(2,128)(2,1)S(1)} %copy.52), channel_id=2, replica_groups=mesh['kv'=8,'seq'=8,'vocab'=4] {'kv'}, dimensions={0}, use_global_device_ids=true | all-gather | bytes 48384 | tf_op jit(solution)/shard_map/all_gather | solution.py:73
  26.3 15.0 %psum.85 = f32[48]{0:T(128)S(1)} all-reduce(f32[48]{0:T(128)S(1)} %fusion.56), channel_id=1, replica_groups=mesh['kv'=8,'seq'=8,'vocab'=4] {'seq'}, use_global_device_ids=true, to_apply=%region_4.5 | all-reduce | flops 48 | bytes 384 | tf_op jit(solution)/shard_map/psum | solution.py:79
  43.9 50.6 %all-reduce.10.cloned.1.call-done = f32[48,1,1024]{2,0,1:T(8,128)} async-done(((f32[48,1,1024]{2,0,1:T(8,128)}), f32[48,1,1024]{2,0,1:T(8,128)}) %all-reduce.10.cloned.1.call-update) | async-done | bytes 196624 | tf_op jit(solution)/shard_map/psum | solution.py:79
  97.1 12.7 %psum.87 = f32[48,1,2]{0,2,1:T(2,128)S(1)} all-reduce(f32[48,1,2]{0,2,1:T(2,128)S(1)} %bitcast.224), channel_id=1, replica_groups=mesh['kv'=8,'seq'=8,'vocab'=4] {'seq'}, use_global_device_ids=true, to_apply=%region_8.9 | all-reduce | flops 96 | bytes 768 | tf_op jit(solution)/shard_map/psum | solution.py:108
  112.0 73.8 %all-reduce.12.cloned.1.call-done = f32[48,1,2,256]{3,0,2,1:T(8,128)} async-done(((f32[48,1,2,256]{3,0,2,1:T(8,128)}), f32[48,1,2,256]{3,0,2,1:T(8,128)}) %all-reduce.12.cloned.1.call-update) | async-done | bytes 98320 | tf_op jit(solution)/shard_map/psum | solution.py:108
  187.3 18.1 %fusion = f32[8,448]{1,0:T(8,128)S(1)} fusion(f32[48,448]{1,0:T(8,128)S(1)} %fusion.35), kind=kCustom, calls=%all-reduce-scatter | all-reduce-scatter fusion | flops 28673 | bytes 101376
  212.0 11.6 %psum.88 = f32[6]{0:T(128)S(1)} all-reduce(f32[6]{0:T(128)S(1)} %multiply_reduce_fusion.2), channel_id=1, replica_groups=mesh['kv'=8,'seq'=8,'vocab'=4] {'seq'}, use_global_device_ids=true, to_apply=%region_12.13 | all-reduce | flops 6 | bytes 48 | tf_op jit(solution)/shard_map/psum | solution.py:36
  223.7 45.5 %all-gather.1 = bf16[32,6,448]{2,1,0:T(8,128)(2,1)S(1)} all-gather(bf16[1,6,448]{2,1,0:T(8,128)(2,1)S(1)} %bitcast.223), channel_id=1, replica_groups=mesh['kv'=8,'seq'=8,'vocab'=4] {'kv','vocab'}, dimensions={0}, use_global_device_ids=true | all-gather | bytes 177408 | tf_op jit(solution)/shard_map/all_gather | solution.py:136
  270.8 11.5 %psum.90 = f32[192]{0:T(256)S(1)} all-reduce(f32[192]{0:T(256)S(1)} %multiply_reduce_fusion), channel_id=1, replica_groups=mesh['kv'=8,'seq'=8,'vocab'=4] {'seq'}, use_global_device_ids=true, to_apply=%region_15.16 | all-reduce | flops 192 | bytes 1536 | tf_op jit(solution)/shard_map/psum | solution.py:143
  282.3 57.1 %all-reduce.14.cloned.1.call-done = f32[192,2,448]{2,0,1:T(8,128)} async-done(((f32[192,2,448]{2,0,1:T(8,128)}), f32[192,2,448]{2,0,1:T(8,128)}) %all-reduce.14.cloned.1.call-update) | async-done | bytes 688144 | tf_op jit(solution)/shard_map/psum | solution.py:143
  341.1 68.1 %fusion.1 = f32[8,448]{1,0:T(8,128)S(1)} fusion(f32[192,448]{1,0:T(8,128)S(1)} %fusion.53), kind=kCustom, calls=%all-reduce-scatter.1 | all-reduce-scatter fusion | flops 114689 | bytes 359424
  418.3 5.9 collective-permute-start.6
  424.2 6.8 collective-permute-start.7
  431.0 3.9 collective-permute-start.8
  437.2 12.6 %psum.91 = f32[6]{0:T(128)S(1)} all-reduce(f32[6]{0:T(128)S(1)} %multiply_reduce_fusion.1), channel_id=1, replica_groups=mesh['kv'=8,'seq'=8,'vocab'=4] {'seq'}, use_global_device_ids=true, to_apply=%region_18.19 | all-reduce | flops 6 | bytes 48 | tf_op jit(solution)/shard_map/psum | solution.py:36
  450.0 10.7 %psum.92 = f32[6]{0:T(128)S(1)} all-reduce(f32[6]{0:T(128)S(1)} %get-tuple-element.17), channel_id=1, replica_groups=mesh['kv'=8,'seq'=8,'vocab'=4] {'seq'}, use_global_device_ids=true, to_apply=%region_20.21 | all-reduce | flops 6 | bytes 48 | tf_op jit(solution)/shard_map/psum | solution.py:36
  460.8 48.2 %all-gather.2 = bf16[32,6,448]{2,1,0:T(8,128)(2,1)S(1)} all-gather(bf16[1,6,448]{2,1,0:T(8,128)(2,1)S(1)} %fusion.82), channel_id=1, replica_groups=mesh['kv'=8,'seq'=8,'vocab'=4] {'kv','vocab'}, dimensions={0}, use_global_device_ids=true | all-gather | bytes 177408 | tf_op jit(solution)/shard_map/all_gather | solution.py:157
  511.2 64.1 %all-reduce.16.cloned.1.call-done = bf16[192,4,112]{2,0,1:T(8,128)(2,1)} async-done(((bf16[192,4,112]{2,0,1:T(8,128)(2,1)}), bf16[192,4,112]{2,0,1:T(8,128)(2,1)}) %all-reduce.16.cloned.1.call-update) | async-done | bytes 172048 | tf_op jit(solution)/shard_map/psum | solution.py:159
  585.5 30.5 %all-gather.9.cloned.1.call-done = bf16[8,448,192]{1,2,0:T(8,128)(2,1)} async-done(((bf16[1,448,192]{1,2,0:T(8,128)(2,1)}), bf16[8,448,192]{1,2,0:T(8,128)(2,1)}) %all-gather.9.cloned.1.call-update) | async-done | bytes 1376272 | tf_op jit(solution)/shard_map/all_gather | solution.py:166
  621.1 3.8 fusion.95
  625.0 52.4 %all-gather.7.cloned.1.call-done = bf16[192,4,3584]{0,1,2:T(4,128)(2,1)} async-done(((bf16[192,4,112]{0,1,2:T(4,128)(2,1)}), bf16[192,4,3584]{0,1,2:T(4,128)(2,1)}) %all-gather.7.cloned.1.call-update) | async-done | bytes 5505040 | tf_op jit(solution)/shard_map/all_gather | solution.py:174
  677.3 8.2 %fusion.17 = f32[192,4,512]{2,0,1:T(8,128)S(1)} fusion(bf16[512,3584]{1,0:T(8,128)(2,1)} %param.36, bf16[192,4,3584]{0,1,2:T(4,128)(2,1)} %all-gather.7.cloned.1.call-done, f32[192,512]{1,0:T(8,128)S(1)} %fusion.95), kind=kOutput, calls=%fused_computation.38 | convolution fusion | flops 2818965504 | bytes 11141120 | tf_op jit(solution)/shard_map/tnc,vc->tnv/dot_general | solution.py:172
  685.6 4.4 select_reduce_fusion
  691.4 76.6 %all-reduce.4 = (f32[192,5]{0,1:T(8,128)S(1)}, f32[5,48,4,8]{1,3,2,0:T(8,128)}) all-reduce(f32[192,5]{0,1:T(8,128)S(1)} %get-tuple-element.19, f32[5,48,4,8]{1,3,2,0:T(8,128)S(1)} %reshape.401), channel_id=1, replica_groups=mesh['kv'=8,'seq'=8,'vocab'=4] {'kv','seq','vocab'}, use_global_device_ids=true, to_apply=%region_23.24 | all-reduce | flops 8640 | bytes 69120 | tf_op jit(solution)/shard_map/psum | solution.py:200
  (158 shorter events, 51.0 us)
Async XLA Ops:
  7.2 262.2 %copy-start = (bf16[448,2,448]{2,1,0:T(2,128)(2,1)S(1)}, bf16[448,2,448]{2,1,0:T(2,128)(2,1)}, u32[]{:S(2)}) copy-start(bf16[448,2,448]{2,1,0:T(2,128)(2,1)} %param.32) | copy-start | bytes 2408452
  7.2 87.3 %all-reduce.10.cloned.1.call-start = ((), (), s32[]{:S(2)}) async-start(), calls=%async_computation | async-start | bytes 393216 | tf_op jit(solution)/shard_map/psum | solution.py:79
  26.2 159.7 %all-reduce.12.cloned.1.call-start = ((), (), s32[]{:S(2)}) async-start(), calls=%async_computation.1 | async-start | bytes 196608 | tf_op jit(solution)/shard_map/psum | solution.py:108
  109.8 159.6 %copy-start.14 = (f32[448]{0:T(512)S(1)}, f32[448]{0:T(512)}, u32[]{:S(2)}) copy-start(f32[448]{0:T(512)} %param.24) | copy-start | bytes 5380
  111.8 227.7 %all-reduce.14.cloned.1.call-start = ((), (), s32[]{:S(2)}) async-start(), calls=%async_computation.2 | async-start | bytes 1572864 | tf_op jit(solution)/shard_map/psum | solution.py:143
  205.3 6.3 collective-permute-start
  208.8 2.8 collective-permute-start.1
  270.6 164.4 %copy-start.19 = (u32[256]{0:T(256)S(1)}, u32[256]{0:T(256)}, u32[]{:S(2)}) copy-start(u32[256]{0:T(256)} %constant.91) | copy-start | bytes 3076
  270.6 179.2 %copy-start.17 = (f32[448]{0:T(512)S(1)}, f32[448]{0:T(512)}, u32[]{:S(2)}) copy-start(f32[448]{0:T(512)} %param.25) | copy-start | bytes 5380
  270.6 190.1 %copy-start.18 = (f32[448]{0:T(512)S(1)}, f32[448]{0:T(512)}, u32[]{:S(2)}) copy-start(f32[448]{0:T(512)} %param.26) | copy-start | bytes 5380
  270.6 238.5 %copy-start.4 = (bf16[4,448,112]{2,1,0:T(8,128)(2,1)S(1)}, bf16[4,448,112]{2,1,0:T(8,128)(2,1)}, u32[]{:S(2)}) copy-start(bf16[4,448,112]{2,1,0:T(8,128)(2,1)} %param.34) | copy-start | bytes 1204228
  270.7 304.6 %all-reduce.16.cloned.1.call-start = ((), (), s32[]{:S(2)}) async-start(), calls=%async_computation.3 | async-start | bytes 393216 | tf_op jit(solution)/shard_map/psum | solution.py:159
  341.1 234.2 %copy-start.15 = (f32[4,112]{1,0:T(4,128)S(1)}, f32[4,112]{1,0:T(4,128)}, u32[]{:S(2)}) copy-start(f32[4,112]{1,0:T(4,128)} %param.35) | copy-start | bytes 5380
  409.1 15.1 %collective-permute-start.2 = (f32[8,448]{1,0:T(8,128)S(1)}, f32[8,448]{1,0:T(8,128)S(1)}, u32[]{:S(2)}, u32[]{:S(2)}) collective-permute-start(f32[8,448]{1,0:T(8,128)S(1)} %fusion.1), channel_id=1, source_target_pairs={{0,1},{1,2},{2,3},{3,32},{32,33},{33,34},{34,35},{35,64},{64,65},{... | collective-permute-start | bytes 43016
  411.1 20.0 %collective-permute-start.3 = (f32[8,448]{1,0:T(8,128)S(1)}, f32[8,448]{1,0:T(8,128)S(1)}, u32[]{:S(2)}, u32[]{:S(2)}) collective-permute-start(f32[8,448]{1,0:T(8,128)S(1)} %fusion.1), channel_id=1, source_target_pairs={{0,2},{1,3},{2,32},{3,33},{32,34},{33,35},{34,64},{35,65},{64,66},... | collective-permute-start | bytes 43016
  413.0 164.3 %copy-start.5 = (s32[5,48,4,8]{1,3,2,0:T(8,128)S(1)}, s32[5,48,4,8]{1,3,2,0:T(8,128)}, u32[]{:S(2)}) copy-start(s32[5,48,4,8]{1,3,2,0:T(8,128)} %param.37) | copy-start | bytes 92164
  413.0 5.3 collective-permute-start.9
  414.4 21.8 %collective-permute-start.4 = (f32[8,448]{1,0:T(8,128)S(1)}, f32[8,448]{1,0:T(8,128)S(1)}, u32[]{:S(2)}, u32[]{:S(2)}) collective-permute-start(f32[8,448]{1,0:T(8,128)S(1)} %fusion.1), channel_id=1, source_target_pairs={{0,3},{1,32},{2,33},{3,34},{32,35},{33,64},{34,65},{35,66},{64,67}... | collective-permute-start | bytes 43016
  416.4 19.9 %collective-permute-start.5 = (f32[8,448]{1,0:T(8,128)S(1)}, f32[8,448]{1,0:T(8,128)S(1)}, u32[]{:S(2)}, u32[]{:S(2)}) collective-permute-start(f32[8,448]{1,0:T(8,128)S(1)} %fusion.1), channel_id=1, source_target_pairs={{0,32},{1,33},{2,34},{3,35},{32,64},{33,65},{34,66},{35,67},{64,96... | collective-permute-start | bytes 43016
  418.3 17.9 %collective-permute-start.6 = (f32[8,448]{1,0:T(8,128)S(1)}, f32[8,448]{1,0:T(8,128)S(1)}, u32[]{:S(2)}, u32[]{:S(2)}) collective-permute-start(f32[8,448]{1,0:T(8,128)S(1)} %fusion.1), channel_id=1, source_target_pairs={{0,33},{1,34},{2,35},{3,64},{32,65},{33,66},{34,67},{35,96},{64,97... | collective-permute-start | bytes 43016
  424.2 12.1 %collective-permute-start.7 = (f32[8,448]{1,0:T(8,128)S(1)}, f32[8,448]{1,0:T(8,128)S(1)}, u32[]{:S(2)}, u32[]{:S(2)}) collective-permute-start(f32[8,448]{1,0:T(8,128)S(1)} %fusion.1), channel_id=1, source_target_pairs={{0,34},{1,35},{2,64},{3,65},{32,66},{33,67},{34,96},{35,97},{64,98... | collective-permute-start | bytes 43016
  431.0 5.2 collective-permute-start.8
  510.1 106.0 %all-gather.9.cloned.1.call-start = ((), (), s32[]{:S(2)}) async-start(), calls=%async_computation.5 | async-start | bytes 1769472 | tf_op jit(solution)/shard_map/all_gather | solution.py:166
  511.0 166.3 %all-gather.7.cloned.1.call-start = ((), (), s32[]{:S(2)}) async-start(), calls=%async_computation.4 | async-start | bytes 7569408 | tf_op jit(solution)/shard_map/all_gather | solution.py:174
  (14 other events, 1120.8 us)
Sparse Core Ops, SparseCore 0:
  26.3 68.1 all-reduce.9
  111.9 73.9 all-reduce.11
  270.8 68.6 all-reduce.13
  510.2 65.0 all-reduce.15
  576.9 39.1 all-gather.8
  618.5 58.7 all-gather.6
where the time goes:
time: 777 us; the launch traced here: 776 us
  blocking collectives  346 us (45%)
  waiting for transfers between devices  329 us (42%)
  starting transfers between devices  31.2 us (4%)
  matrix products  26.7 us (3%)
  between operations  16.9 us (2%)
  local copies, waits for them, and re-layouts  16 us (2%)
  other arithmetic  9.93 us (1%)
    unnamed x2, blocking collectives  86.2 us
    psum x1, blocking collectives, local(): totals, picked = lax.psum((totals, picked), ('kv', 'seq', 'vocab'))  76.6 us
    psum x1, waiting for transfers between devices, local(): lax.psum((numerator, jnp.sum(weights, axis=-1)), 'seq')  73.8 us
    psum x1, waiting for transfers between devices, local(): lifted = lax.psum(lifted.astype(jnp.bfloat16), 'seq').astype(jnp.float32)  64.1 us
    psum x1, waiting for transfers between devices, local(): gate_up, ffn_squares = lax.psum((gate_up, ffn_squares), 'seq')  57.1 us
    all_gather x1, waiting for transfers between devices, local(): lax.all_gather(branch, ('kv', 'vocab'), axis=2, tiled=True)  52.4 us
    psum x1, waiting for transfers between devices, local(): lax.psum((projected_rows, jnp.sum(tenant_float * tenant_float, axis=-1)),...  50.6 us
    all_gather x1, blocking collectives, local(): gathered = lax.all_gather(normed, ('kv', 'vocab'), axis=0, tiled=True)  48.2 us
  transfers between devices with their start and end apart: 16, of which 6 were waited for; matrix products, arithmetic and copies ran while one was open for 3% of the time, Pallas kernels for 0%

commit v1 on v0

--- a/solution.py
+++ b/solution.py
@@ -1,3 +1,4 @@
+import functools
 import jax
 import jax.numpy as jnp
 from jax import lax
@@ -9,6 +10,36 @@
 EPSILON = 1e-06
 SCORE_CAP = 50.0
 LOGIT_CAP = 30.0
+
+
+def core_recover(vals, named_axis, k_dim):
+    current_value, front, answer = (
+        lax.axis_size(named_axis),
+        lax.axis_index(named_axis),
+        vals.shape[k_dim],
+    )
+    rows = list(map(lambda m: (m, (m + 1) % current_value), range(current_value)))
+    so_far_all = list(map(lambda m: (m, (m - 1) % current_value), range(current_value)))
+    b_now = jnp.zeros(
+        (*vals.shape[:k_dim], current_value * answer, *vals.shape[k_dim + 1 :]), vals.dtype
+    )
+    b_now = lax.dynamic_update_slice_in_dim(b_now, vals, front * answer, axis=k_dim)
+    raw_out = value_now = vals
+    x_new = current_value // 2
+    for ix in range(1, x_new + 1):
+        raw_out = lax.ppermute(raw_out, axis_name=named_axis, perm=rows)
+        b_now = lax.dynamic_update_slice_in_dim(
+            b_now, raw_out, (front - ix) % current_value * answer, axis=k_dim
+        )
+        if ix < current_value - x_new:
+            value_now = lax.ppermute(value_now, axis_name=named_axis, perm=so_far_all)
+            b_now = lax.dynamic_update_slice_in_dim(
+                b_now, value_now, (front + ix) % current_value * answer, axis=k_dim
+            )
+    return b_now
+
+
+_part_roads = functools.partial(core_recover, named_axis="seq", k_dim=1)
 
 
 def apply_rotary(vectors, token_positions):
@@ -163,10 +194,7 @@
     draft_count = branch.shape[1]
     columns = vocab_weight
     base_logits = lax.dot_general(
-        lax.all_gather(gathered, "seq", axis=1, tiled=True),
-        columns,
-        (((1,), (1,)), ((), ())),
-        preferred_element_type=jnp.float32,
+        _part_roads(gathered), columns, (((1,), (1,)), ((), ())), preferred_element_type=jnp.float32
     )
     columns = vocab_weight
     draft_extra = jnp.einsum(

time: 777 us -> 743 us (0.956)
  waiting for transfers between devices: 329 us -> 262 us
  local copies, waits for them, and re-layouts: 16 us -> 37.1 us
    all_gather x1, waiting for transfers between devices: 52.4 us -> 2.18 us  [local(): lax.all_gather(branch, ('kv', 'vocab'), axis=2, tiled=True)]
    all_gather x1 -> x0, waiting for transfers between devices: 30.5 us -> none  [local(): lax.all_gather(gathered, 'seq', axis=1, tiled=True)]
    dynamic_update_slice x0 -> x8, local copies, waits for them, and re-layouts: none -> 24.8 us  [the longest x4 12.1 us: core_recover(): lax.dynamic_update_slice_in_dim(b_now, raw_out, (front - ix) % current_va...]
    ppermute x0 -> x7, waiting for transfers between devices: none -> 9.1 us  [the longest x4 8.41 us: core_recover(): raw_out = lax.ppermute(raw_out, axis_name=named_axis, perm=rows)]
    ppermute x0 -> x7, starting transfers between devices: none -> 8.61 us  [the longest x3 7.77 us: core_recover(): value_now = lax.ppermute(value_now, axis_name=named_axis, perm=so_far_all)]
  transfers between devices with their start and end apart: 16 -> 22, of which waited for: 6 -> 10; matrix products, arithmetic and copies ran while one was open for 3% -> 6% of each run, Pallas kernels for 0% -> 0%
where the time goes in v1:
time: 743 us; the launch traced here: 742 us
  blocking collectives  350 us (47%)
  waiting for transfers between devices  262 us (35%)
  starting transfers between devices  38.4 us (5%)
  local copies, waits for them, and re-layouts  37.1 us (5%)
  matrix products  26.9 us (4%)
  between operations  16.6 us (2%)
  other arithmetic  10.6 us (1%)
    unnamed x2, blocking collectives  86.2 us
    psum x1, blocking collectives, local(): totals, picked = lax.psum((totals, picked), ('kv', 'seq', 'vocab'))  82.8 us
    psum x1, waiting for transfers between devices, local(): lax.psum((numerator, jnp.sum(weights, axis=-1)), 'seq')  73.8 us
    psum x1, waiting for transfers between devices, local(): lifted = lax.psum(lifted.astype(jnp.bfloat16), 'seq').astype(jnp.float32)  66 us
    psum x1, waiting for transfers between devices, local(): gate_up, ffn_squares = lax.psum((gate_up, ffn_squares), 'seq')  57.1 us
    psum x1, waiting for transfers between devices, local(): lax.psum((projected_rows, jnp.sum(tenant_float * tenant_float, axis=-1)),...  50.6 us
    all_gather x1, blocking collectives, local(): gathered = lax.all_gather(normed, ('kv', 'vocab'), axis=0, tiled=True)  45.8 us
    all_gather x1, blocking collectives, local(): all_state = lax.all_gather(first_sum, ('kv', 'vocab'), axis=0, tiled=True)  45.5 us
  transfers between devices with their start and end apart: 22, of which 10 were waited for; matrix products, arithmetic and copies ran while one was open for 6% of the time, Pallas kernels for 0%

profile of v1, /device:TPU:1, one launch (start us, length us, event | category | flops | bytes accessed | tf_op | source)
XLA Modules:
  0.0 741.7 jit_solution(621480224853497654)
XLA Ops:
  8.1 15.8 %all-gather = bf16[48,1,448]{2,1,0:T(2,128)(2,1)S(1)} all-gather(bf16[6,1,448]{2,1,0:T(2,128)(2,1)S(1)} %copy.50), channel_id=2, replica_groups=mesh['kv'=8,'seq'=8,'vocab'=4] {'kv'}, dimensions={0}, use_global_device_ids=true | all-gather | bytes 48384 | tf_op jit(solution)/shard_map/all_gather | solution.py:104
  26.3 15.0 %psum.85 = f32[48]{0:T(128)S(1)} all-reduce(f32[48]{0:T(128)S(1)} %fusion.51), channel_id=1, replica_groups=mesh['kv'=8,'seq'=8,'vocab'=4] {'seq'}, use_global_device_ids=true, to_apply=%region_4.5 | all-reduce | flops 48 | bytes 384 | tf_op jit(solution)/shard_map/psum | solution.py:110
  43.9 50.6 %all-reduce.10.cloned.1.call-done = f32[48,1,1024]{2,0,1:T(8,128)} async-done(((f32[48,1,1024]{2,0,1:T(8,128)}), f32[48,1,1024]{2,0,1:T(8,128)}) %all-reduce.10.cloned.1.call-update) | async-done | bytes 196624 | tf_op jit(solution)/shard_map/psum | solution.py:110
  97.1 12.7 %psum.87 = f32[48,1,2]{0,2,1:T(2,128)S(1)} all-reduce(f32[48,1,2]{0,2,1:T(2,128)S(1)} %bitcast.218), channel_id=1, replica_groups=mesh['kv'=8,'seq'=8,'vocab'=4] {'seq'}, use_global_device_ids=true, to_apply=%region_8.9 | all-reduce | flops 96 | bytes 768 | tf_op jit(solution)/shard_map/psum | solution.py:139
  112.1 73.8 %all-reduce.12.cloned.1.call-done = f32[48,1,2,256]{3,0,2,1:T(8,128)} async-done(((f32[48,1,2,256]{3,0,2,1:T(8,128)}), f32[48,1,2,256]{3,0,2,1:T(8,128)}) %all-reduce.12.cloned.1.call-update) | async-done | bytes 98320 | tf_op jit(solution)/shard_map/psum | solution.py:139
  187.3 18.1 %fusion = f32[8,448]{1,0:T(8,128)S(1)} fusion(f32[48,448]{1,0:T(8,128)S(1)} %fusion.30), kind=kCustom, calls=%all-reduce-scatter | all-reduce-scatter fusion | flops 28673 | bytes 101376
  212.0 11.6 %psum.88 = f32[6]{0:T(128)S(1)} all-reduce(f32[6]{0:T(128)S(1)} %multiply_reduce_fusion.2), channel_id=1, replica_groups=mesh['kv'=8,'seq'=8,'vocab'=4] {'seq'}, use_global_device_ids=true, to_apply=%region_12.13 | all-reduce | flops 6 | bytes 48 | tf_op jit(solution)/shard_map/psum | solution.py:67
  223.7 45.5 %all-gather.1 = bf16[32,6,448]{2,1,0:T(8,128)(2,1)S(1)} all-gather(bf16[1,6,448]{2,1,0:T(8,128)(2,1)S(1)} %bitcast.217), channel_id=1, replica_groups=mesh['kv'=8,'seq'=8,'vocab'=4] {'kv','vocab'}, dimensions={0}, use_global_device_ids=true | all-gather | bytes 177408 | tf_op jit(solution)/shard_map/all_gather | solution.py:167
  270.8 11.5 %psum.90 = f32[192]{0:T(256)S(1)} all-reduce(f32[192]{0:T(256)S(1)} %multiply_reduce_fusion), channel_id=1, replica_groups=mesh['kv'=8,'seq'=8,'vocab'=4] {'seq'}, use_global_device_ids=true, to_apply=%region_15.16 | all-reduce | flops 192 | bytes 1536 | tf_op jit(solution)/shard_map/psum | solution.py:174
  282.4 57.1 %all-reduce.14.cloned.1.call-done = f32[192,2,448]{2,0,1:T(8,128)} async-done(((f32[192,2,448]{2,0,1:T(8,128)}), f32[192,2,448]{2,0,1:T(8,128)}) %all-reduce.14.cloned.1.call-update) | async-done | bytes 688144 | tf_op jit(solution)/shard_map/psum | solution.py:174
  341.1 68.1 %fusion.1 = f32[8,448]{1,0:T(8,128)S(1)} fusion(f32[192,448]{1,0:T(8,128)S(1)} %fusion.48), kind=kCustom, calls=%all-reduce-scatter.1 | all-reduce-scatter fusion | flops 114689 | bytes 359424
  419.4 7.2 collective-permute-start.14
  426.6 5.3 collective-permute-start.15
  439.1 12.6 %psum.91 = f32[6]{0:T(128)S(1)} all-reduce(f32[6]{0:T(128)S(1)} %multiply_reduce_fusion.1), channel_id=1, replica_groups=mesh['kv'=8,'seq'=8,'vocab'=4] {'seq'}, use_global_device_ids=true, to_apply=%region_18.19 | all-reduce | flops 6 | bytes 48 | tf_op jit(solution)/shard_map/psum | solution.py:67
  451.9 10.7 %psum.92 = f32[6]{0:T(128)S(1)} all-reduce(f32[6]{0:T(128)S(1)} %get-tuple-element.17), channel_id=1, replica_groups=mesh['kv'=8,'seq'=8,'vocab'=4] {'seq'}, use_global_device_ids=true, to_apply=%region_20.21 | all-reduce | flops 6 | bytes 48 | tf_op jit(solution)/shard_map/psum | solution.py:67
  462.7 45.8 %all-gather.2 = bf16[32,6,448]{2,1,0:T(8,128)(2,1)S(1)} all-gather(bf16[1,6,448]{2,1,0:T(8,128)(2,1)S(1)} %fusion.77), channel_id=1, replica_groups=mesh['kv'=8,'seq'=8,'vocab'=4] {'kv','vocab'}, dimensions={0}, use_global_device_ids=true | all-gather | bytes 177408 | tf_op jit(solution)/shard_map/all_gather | solution.py:188
  509.7 66.0 %all-reduce.16.cloned.1.call-done = bf16[192,4,112]{2,0,1:T(8,128)(2,1)} async-done(((bf16[192,4,112]{2,0,1:T(8,128)(2,1)}), bf16[192,4,112]{2,0,1:T(8,128)(2,1)}) %all-reduce.16.cloned.1.call-update) | async-done | bytes 172048 | tf_op jit(solution)/shard_map/psum | solution.py:190
  593.1 4.2 collective-permute-done.2
  611.7 3.6 dynamic_update_slice.26
  621.4 3.6 dynamic_update_slice.29
  625.0 3.6 dynamic_update_slice.30
  637.5 8.2 %broadcast_add_fusion = f32[192,4,512]{2,0,1:T(8,128)S(1)} fusion(f32[192,512]{1,0:T(8,128)S(1)} %fusion.90, bf16[512,3584]{1,0:T(8,128)(2,1)} %param.36, bf16[192,4,3584]{0,1,2:T(4,128)(2,1)} %all-gather.5.cloned.1.call-done), kind=kOutput, calls=%fused_computation.56 | convolution fusion | flops 2818965504 | bytes 11141120 | tf_op jit(solution)/shard_map/tnc,vc->tnv/dot_general | solution.py:200
  645.8 4.4 select_reduce_fusion
  651.5 82.8 %all-reduce.4 = (f32[192,5]{0,1:T(8,128)S(1)}, f32[5,48,4,8]{1,3,2,0:T(8,128)}) all-reduce(f32[192,5]{0,1:T(8,128)S(1)} %get-tuple-element.19, f32[5,48,4,8]{1,3,2,0:T(8,128)S(1)} %reshape.401), channel_id=1, replica_groups=mesh['kv'=8,'seq'=8,'vocab'=4] {'kv','seq','vocab'}, use_global_device_ids=true, to_apply=%region_23.24 | all-reduce | flops 8640 | bytes 69120 | tf_op jit(solution)/shard_map/psum | solution.py:228
  (188 shorter events, 87.3 us)
Async XLA Ops:
  7.2 262.2 %copy-start = (bf16[448,2,448]{2,1,0:T(2,128)(2,1)S(1)}, bf16[448,2,448]{2,1,0:T(2,128)(2,1)}, u32[]{:S(2)}) copy-start(bf16[448,2,448]{2,1,0:T(2,128)(2,1)} %param.32) | copy-start | bytes 2408452
  7.2 87.3 %all-reduce.10.cloned.1.call-start = ((), (), s32[]{:S(2)}) async-start(), calls=%async_computation | async-start | bytes 393216 | tf_op jit(solution)/shard_map/psum | solution.py:110
  26.2 159.7 %all-reduce.12.cloned.1.call-start = ((), (), s32[]{:S(2)}) async-start(), calls=%async_computation.1 | async-start | bytes 196608 | tf_op jit(solution)/shard_map/psum | solution.py:139
  111.8 227.7 %all-reduce.14.cloned.1.call-start = ((), (), s32[]{:S(2)}) async-start(), calls=%async_computation.2 | async-start | bytes 1572864 | tf_op jit(solution)/shard_map/psum | solution.py:174
  205.4 6.3 collective-permute-start.7
  208.8 2.8 collective-permute-start.8
  270.7 305.0 %all-reduce.16.cloned.1.call-start = ((), (), s32[]{:S(2)}) async-start(), calls=%async_computation.3 | async-start | bytes 393216 | tf_op jit(solution)/shard_map/psum | solution.py:190
  282.4 293.3 %copy-start.22 = (f32[4,112]{1,0:T(4,128)S(1)}, f32[4,112]{1,0:T(4,128)}, u32[]{:S(2)}) copy-start(f32[4,112]{1,0:T(4,128)} %param.35) | copy-start | bytes 5380
  409.2 17.4 %collective-permute-start.10 = (f32[8,448]{1,0:T(8,128)S(1)}, f32[8,448]{1,0:T(8,128)S(1)}, u32[]{:S(2)}, u32[]{:S(2)}) collective-permute-start(f32[8,448]{1,0:T(8,128)S(1)} %fusion.1), channel_id=1, source_target_pairs={{0,2},{1,3},{2,32},{3,33},{32,34},{33,35},{34,64},{35,65},{64,66},... | collective-permute-start | bytes 43016
  411.1 20.8 %collective-permute-start.11 = (f32[8,448]{1,0:T(8,128)S(1)}, f32[8,448]{1,0:T(8,128)S(1)}, u32[]{:S(2)}, u32[]{:S(2)}) collective-permute-start(f32[8,448]{1,0:T(8,128)S(1)} %fusion.1), channel_id=1, source_target_pairs={{0,3},{1,32},{2,33},{3,34},{32,35},{33,64},{34,65},{35,66},{64,67}... | collective-permute-start | bytes 43016
  413.0 6.3 collective-permute-start.16
  414.3 20.8 %collective-permute-start.12 = (f32[8,448]{1,0:T(8,128)S(1)}, f32[8,448]{1,0:T(8,128)S(1)}, u32[]{:S(2)}, u32[]{:S(2)}) collective-permute-start(f32[8,448]{1,0:T(8,128)S(1)} %fusion.1), channel_id=1, source_target_pairs={{0,32},{1,33},{2,34},{3,35},{32,64},{33,65},{34,66},{35,67},{64,96... | collective-permute-start | bytes 43016
  416.3 18.8 %collective-permute-start.13 = (f32[8,448]{1,0:T(8,128)S(1)}, f32[8,448]{1,0:T(8,128)S(1)}, u32[]{:S(2)}, u32[]{:S(2)}) collective-permute-start(f32[8,448]{1,0:T(8,128)S(1)} %fusion.1), channel_id=1, source_target_pairs={{0,33},{1,34},{2,35},{3,64},{32,65},{33,66},{34,67},{35,96},{64,97... | collective-permute-start | bytes 43016
  419.4 15.8 %collective-permute-start.14 = (f32[8,448]{1,0:T(8,128)S(1)}, f32[8,448]{1,0:T(8,128)S(1)}, u32[]{:S(2)}, u32[]{:S(2)}) collective-permute-start(f32[8,448]{1,0:T(8,128)S(1)} %fusion.1), channel_id=1, source_target_pairs={{0,34},{1,35},{2,64},{3,65},{32,66},{33,67},{34,96},{35,97},{64,98... | collective-permute-start | bytes 43016
  426.6 8.5 %collective-permute-start.15 = (f32[8,448]{1,0:T(8,128)S(1)}, f32[8,448]{1,0:T(8,128)S(1)}, u32[]{:S(2)}, u32[]{:S(2)}) collective-permute-start(f32[8,448]{1,0:T(8,128)S(1)} %fusion.1), channel_id=1, source_target_pairs={{0,35},{1,64},{2,65},{3,66},{32,67},{33,96},{34,97},{35,98},{64,99... | collective-permute-start | bytes 43016
  431.9 6.3 collective-permute-start.9
  509.6 127.8 %all-gather.5.cloned.1.call-start = ((), (), s32[]{:S(2)}) async-start(), calls=%async_computation.4 | async-start | bytes 7569408 | tf_op jit(solution)/shard_map/all_gather | solution.py:202
  583.5 5.8 collective-permute-start
  585.4 4.6 collective-permute-start.1
  589.3 8.0 %collective-permute-start.2 = (bf16[192,448]{1,0:T(8,128)(2,1)S(1)}, bf16[192,448]{1,0:T(8,128)(2,1)S(1)}, u32[]{:S(2)}, u32[]{:S(2)}) collective-permute-start(bf16[192,448]{1,0:T(8,128)(2,1)S(1)} %collective-permute-done), channel_id=1, source_target_pairs={{0,4},{4,8},{8,12},{12,16},{16,20},{20,24},{24,28},{28,0},{1,5},{5... | collective-permute-start | bytes 516104 | tf_op jit(solution)/shard_map/ppermute | solution.py:30
  590.0 9.6 %collective-permute-start.3 = (bf16[192,448]{1,0:T(8,128)(2,1)S(1)}, bf16[192,448]{1,0:T(8,128)(2,1)}, u32[]{:S(2)}, u32[]{:S(2)}) collective-permute-start(bf16[192,448]{1,0:T(8,128)(2,1)S(1)} %collective-permute-done.1), channel_id=1, source_target_pairs={{0,28},{4,0},{8,4},{12,8},{16,12},{20,16},{24,20},{28,24},{1,29},{... | collective-permute-start | bytes 516104 | tf_op jit(solution)/shard_map/ppermute | solution.py:35
  597.2 7.3 collective-permute-start.4
  599.6 25.5 %collective-permute-start.5 = (bf16[192,448]{1,0:T(8,128)(2,1)}, bf16[192,448]{1,0:T(8,128)(2,1)}, u32[]{:S(2)}, u32[]{:S(2)}) collective-permute-start(bf16[192,448]{1,0:T(8,128)(2,1)} %collective-permute-done.3), channel_id=1, source_target_pairs={{0,28},{4,0},{8,4},{12,8},{16,12},{20,16},{24,20},{28,24},{1,29},{... | collective-permute-start | bytes 516104 | tf_op jit(solution)/shard_map/ppermute | solution.py:35
  604.5 24.1 %collective-permute-start.6 = (bf16[192,448]{1,0:T(8,128)(2,1)}, bf16[192,448]{1,0:T(8,128)(2,1)}, u32[]{:S(2)}, u32[]{:S(2)}) collective-permute-start(bf16[192,448]{1,0:T(8,128)(2,1)} %collective-permute-done.4), channel_id=1, source_target_pairs={{0,4},{4,8},{8,12},{12,16},{16,20},{20,24},{24,28},{28,0},{1,5},{5... | collective-permute-start | bytes 516104 | tf_op jit(solution)/shard_map/ppermute | solution.py:30
  (26 other events, 2212.1 us)
Sparse Core Ops, SparseCore 0:
  26.3 68.1 all-reduce.9
  111.9 73.9 all-reduce.11
  270.8 68.6 all-reduce.13
  509.7 65.8 all-reduce.15
  578.1 59.2 all-gather.4
